TPU v7x, 256 devices: a whole 4x4x8 slice. The times are simulated.
256 devices in a mesh: acq: 32 (over z, x_lo, core), strip: 8 (over x_hi, y).
Axes of the slice: x: 4 (x_hi: 2, x_lo: 2; x = x_hi * 2 + x_lo), y: 4, z: 8, core: 2. Of those that a mesh axis runs over, the one named last changes fastest.
Arguments:
- echoes: float32 [128, 2, 256, 2048], P('acq', None, 'strip'), may hold values from -12 to 12
- pair_list: int32 [128, 2], P('acq'), may hold values from 0 to 127, as said below
- phase_ramps: int32 [128, 2], P('acq'), may hold values from -4 to 4
Outputs:
- coherence: float32 [128, 2, 256, 128], P('acq', None, 'strip')
Inputs may be any that keep to these rules, and one draw needn't show every extreme that they name: `pair_list`: row p's secondary lies in block p // 4 of 4 acquisitions (acquisitions k * 4 to k * 4 + 3 form block k), and every acquisition of that block is the secondary of 1 of its rows, in order of row. The reference differs from the secondary; in block 0 it lies in block 0, elsewhere it is 1 to 3 acquisitions before the secondary. The first acquisition of every block but block 0 has its reference in the block before.
All inputs are finite; a program needn't handle non-finite values.
Results may differ from a plain program's by a relative error of at most 0.0003.
Values sent between devices are 32-bit elements; how exact they have to be, the bound alone decides.
A program may use at most 64 MiB of HBM per device.

v0:
```python
import math

import jax
import jax.numpy as jnp
from jax import lax
from jax.sharding import PartitionSpec as P


def passed_along(block, axis, distance):
    devices = range(lax.axis_size(axis))
    route = [(i - distance, i) for i in devices if i - distance in devices]
    return lax.ppermute(block, axis, route)


def with_halo(value, sides, width):
    for axis, dim in sides:
        size, length = (lax.axis_size(axis), value.shape[dim])
        up = [(i, (i + 1) % size) for i in range(size - 1)]
        down = [(j, i) for i, j in up]
        last = lax.slice_in_dim(value, length - width, length, axis=dim)
        initial = lax.slice_in_dim(value, 0, width, axis=dim)
        before = lax.ppermute(last, axis, up)
        after = lax.ppermute(initial, axis, down)
        value = jnp.concatenate([before, value, after], axis=dim)
    return value


def range_taps():
    offsets = jnp.arange(64, dtype=jnp.int32) - 32
    shifted = offsets.astype(jnp.float32) + 0.5
    return jnp.exp(-(shifted * shifted) / 512.0).reshape(4, 16)


def azimuth_band(line_rows):
    out_ids = jnp.arange(line_rows, dtype=jnp.int32)[:, None]
    in_ids = jnp.arange(line_rows + 16, dtype=jnp.int32)[None, :]
    offsets = in_ids - out_ids - 8
    values = offsets.astype(jnp.float32)
    inside = (offsets >= -8) & (offsets <= 8)
    return jnp.where(inside, jnp.exp(-(values * values) / 32.0), 0.0)


def interfere(
    first_piece, second_piece, ramp_pair, line_index, range_index, range_count, line_count
):
    real_first, imag_first = (first_piece[0], first_piece[1])
    real_second, imag_second = (second_piece[0], second_piece[1])
    real_part = real_first * real_second + imag_first * imag_second
    imag_part = imag_first * real_second - real_first * imag_second
    range_turns = jnp.mod(ramp_pair[0] * range_index, range_count).astype(jnp.float32) / float(
        range_count
    )
    line_turns = jnp.mod(ramp_pair[1] * line_index, line_count).astype(jnp.float32) / float(
        line_count
    )
    angles = 2.0 * math.pi * (range_turns[None, :] + line_turns[:, None])
    cosine = jnp.cos(angles)
    sine = jnp.sin(angles)
    return jnp.stack(
        [
            real_part * cosine + imag_part * sine,
            imag_part * cosine - real_part * sine,
            real_first * real_first + imag_first * imag_first,
            real_second * real_second + imag_second * imag_second,
        ]
    )


def range_look(fields):
    outputs = fields.shape[2] // 16
    blocked = fields.reshape(fields.shape[0], fields.shape[1], outputs, 16)
    blocked = jnp.pad(blocked, ((0, 0), (0, 0), (2, 2), (0, 0)))
    tap_weights = range_taps()
    summed = jnp.zeros((fields.shape[0], fields.shape[1], outputs), jnp.float32)
    for offset in range(4):
        summed = summed + jnp.einsum(
            "flok,k->flo",
            blocked[:, :, offset : offset + outputs, :],
            tap_weights[offset],
            precision=lax.Precision.HIGHEST,
        )
    return summed


def pair_looks(stacked, ref_index, sec_index, phase_ramps, first_line, line_count):
    line_rows = stacked.shape[2]
    range_width = stacked.shape[3]
    range_index = jnp.arange(range_width, dtype=jnp.int32)
    line_index = first_line + jnp.arange(line_rows, dtype=jnp.int32)

    def per_pair(items):
        first_slot, second_slot, ramp_pair = items
        first_piece = lax.dynamic_index_in_dim(stacked, first_slot, 0, keepdims=False)
        second_piece = lax.dynamic_index_in_dim(stacked, second_slot, 0, keepdims=False)
        fields = interfere(
            first_piece, second_piece, ramp_pair, line_index, range_index, range_width, line_count
        )
        return range_look(fields)

    return lax.map(per_pair, (ref_index, sec_index, phase_ramps))


def body(echoes, pair_list, phase_ramps):
    acq_count = echoes.shape[0]
    line_rows = echoes.shape[2]
    position = lax.axis_index("acq")
    strip_pos = lax.axis_index("strip")
    line_count = lax.axis_size("strip") * line_rows
    ref_index = pair_list[:, 0] - (position - 1) * acq_count
    sec_index = pair_list[:, 1] - position * acq_count + acq_count
    previous = passed_along(echoes, "acq", 1)
    stacked = jnp.concatenate([previous, echoes], axis=0)
    looked = pair_looks(
        stacked, ref_index, sec_index, phase_ramps, strip_pos * line_rows, line_count
    )
    looked = with_halo(looked, (("strip", 2),), 8)
    band = azimuth_band(line_rows)
    summed = jnp.einsum("lm,pkmo->pklo", band, looked, precision=lax.Precision.HIGHEST)
    scaling = 1.0 / jnp.sqrt(summed[:, 2] * summed[:, 3] + 1e-06)
    return jnp.stack([summed[:, 0] * scaling, summed[:, 1] * scaling], axis=1)


def solution(mesh):
    return jax.shard_map(
        body,
        mesh=mesh,
        in_specs=(P("acq", None, "strip", None), P("acq", None), P("acq", None)),
        out_specs=P("acq", None, "strip", None),
        check_vma=False,
    )
```

profile of v0, /device:TPU:184, one launch (start us, length us, event | category | flops | bytes accessed | tf_op | source)
XLA Modules:
  0.0 143.0 jit_solution(15875507636171080816)
XLA Ops:
  0.0 1.9 %collective-permute-start = (f32[4,2,32,2048]{3,2,1,0:T(8,128)}, f32[4,2,32,2048]{3,2,1,0:T(8,128)S(1)}, u32[]{:S(2)}, u32[]{:S(2)}) collective-permute-start(f32[4,2,32,2048]{3,2,1,0:T(8,128)} %param.5), channel_id=1, source_target_pairs={{0,8},{8,16},{16,24},{24,32},{32,40},{40,48},{48,56},{56,64},{64,7... | collective-permute-start | bytes 6291464 | tf_op jit(solution)/shard_map/ppermute | solution.py:12
  1.9 0.8 add_bitcast_fusion
  2.7 25.8 %collective-permute-done = f32[4,2,32,2048]{3,2,1,0:T(8,128)S(1)} collective-permute-done((f32[4,2,32,2048]{3,2,1,0:T(8,128)}, f32[4,2,32,2048]{3,2,1,0:T(8,128)S(1)}, u32[]{:S(2)}, u32[]{:S(2)}) %collective-permute-start) | collective-permute-done | bytes 2097184 | tf_op jit(solution)/shard_map/ppermute | solution.py:12
  28.5 3.9 %pad_maximum_fusion.2 = f32[8,2,32,2048]{3,2,1,0:T(8,128)} fusion(f32[4,2,32,2048]{3,2,1,0:T(8,128)} %param.5, f32[4,2,32,2048]{3,2,1,0:T(8,128)S(1)} %collective-permute-done), kind=kLoop, calls=%fused_computation.47 | loop fusion | flops 1048576 | bytes 8388608 | tf_op jit(solution)/shard_map/concatenate | solution.py:112
  32.4 10.4 %copy.18 = f32[8,2,32,2048]{2,3,1,0:T(8,128)} copy(f32[8,2,32,2048]{3,2,1,0:T(8,128)} %pad_maximum_fusion.2) | data formatting | bytes 8388608
  42.8 82.9 %while.14 = (s32[]{:T(128)}, f32[4,4,32,128]{3,2,1,0:T(8,128)}, s32[4]{0:T(128)S(1)}, f32[8,2,32,2048]{2,3,1,0:T(8,128)}, s32[4]{0:T(128)S(1)}, /*index=5*/s32[4...) while((s32[]{:T(128)}, f32[4,4,32,128]{3,2,1,0:T(8,128)}, ...), condition=%wide.region_1.2_spmd.clone, body=%wide.region_0.1_spmd.clone.sunk | while | flops 15545193 | bytes 12192017 | solution.py:100
  42.8 0.6 dynamic_slice.49
  45.3 0.6 dynamic_slice.48
  47.8 3.6 %multiply_subtract_fusion.3 = (f32[1,1,32,2048]{2,3,1,0:T(8,128)}, f32[1,1,32,2048]{2,3,1,0:T(8,128)S(1)}, f32[1,1,32,2048]{2,3,1,0:T(8,128)S(1)}, f32[1,1,32,2048]{2,3,1,0:T(8,128)S(1)}) fusion(f32[8,2,32,2048]{2,3,1,0:T(8,128)} %get-tuple-element.285, s32[]{:T(128)S(6)} %select_n.77, s32[]{:T(128)S(6)} %select_n.78, s32[]{:T(128)S(6)} %add.343), kind=kLoop, calls=%fused_computation.11.clone.1 | loop fusion | flops 786432 | bytes 2097164 | tf_op jit(solution)/shard_map/while/body/eval_jaxpr/sub | solution.py:49
  51.4 1.7 %copy.35 = f32[1,32,128,16]{2,3,1,0:T(8,128)S(1)} copy(f32[1,32,128,16]{1,3,2,0:T(8,128)} %bitcast.86) | data formatting | bytes 524288 | tf_op jit(solution)/shard_map/while/body/eval_jaxpr/sub | solution.py:49
  53.1 1.2 copy.36
  54.9 0.7 fusion.72
  55.7 0.7 iota_multiply_fusion.2
  56.5 2.1 %multiply_add_fusion.5 = (f32[1,32,128,16]{2,3,1,0:T(8,128)S(1)}, f32[1,32,128,16]{2,3,1,0:T(8,128)S(1)}) fusion(f32[1,32,128,16]{2,3,1,0:T(8,128)S(1)} %copy.35, f32[1,32,128,16]{2,3,1,0:T(8,128)} %copy.36, f32[32]{0:T(128)S(1)} %fusion.72, f32[128,16]{0,1:T(8,128)S(1)} %copy.37), kind=kLoop, calls=%fused_computation.14.clone.1 | loop fusion | flops 524288 | bytes 1056896 | tf_op jit(solution)/shard_map/while/body/eval_jaxpr/add | solution.py:61
  59.6 0.7 fusion.75
  60.4 0.8 fusion.74
  61.2 0.8 fusion.76
  62.0 0.8 fusion.77
  62.9 0.7 bitcast_dynamic-update-slice_fusion.2
  63.5 0.6 dynamic_slice.49
  66.0 0.6 dynamic_slice.48
  68.5 3.6 %multiply_subtract_fusion.3 = (f32[1,1,32,2048]{2,3,1,0:T(8,128)}, f32[1,1,32,2048]{2,3,1,0:T(8,128)S(1)}, f32[1,1,32,2048]{2,3,1,0:T(8,128)S(1)}, f32[1,1,32,2048]{2,3,1,0:T(8,128)S(1)}) fusion(f32[8,2,32,2048]{2,3,1,0:T(8,128)} %get-tuple-element.285, s32[]{:T(128)S(6)} %select_n.77, s32[]{:T(128)S(6)} %select_n.78, s32[]{:T(128)S(6)} %add.343), kind=kLoop, calls=%fused_computation.11.clone.1 | loop fusion | flops 786432 | bytes 2097164 | tf_op jit(solution)/shard_map/while/body/eval_jaxpr/sub | solution.py:49
  72.1 1.7 %copy.35 = f32[1,32,128,16]{2,3,1,0:T(8,128)S(1)} copy(f32[1,32,128,16]{1,3,2,0:T(8,128)} %bitcast.86) | data formatting | bytes 524288 | tf_op jit(solution)/shard_map/while/body/eval_jaxpr/sub | solution.py:49
  73.8 1.2 copy.36
  75.7 0.7 fusion.72
  76.4 0.7 iota_multiply_fusion.2
  77.3 2.1 %multiply_add_fusion.5 = (f32[1,32,128,16]{2,3,1,0:T(8,128)S(1)}, f32[1,32,128,16]{2,3,1,0:T(8,128)S(1)}) fusion(f32[1,32,128,16]{2,3,1,0:T(8,128)S(1)} %copy.35, f32[1,32,128,16]{2,3,1,0:T(8,128)} %copy.36, f32[32]{0:T(128)S(1)} %fusion.72, f32[128,16]{0,1:T(8,128)S(1)} %copy.37), kind=kLoop, calls=%fused_computation.14.clone.1 | loop fusion | flops 524288 | bytes 1056896 | tf_op jit(solution)/shard_map/while/body/eval_jaxpr/add | solution.py:61
  80.3 0.7 fusion.75
  81.1 0.8 fusion.74
  82.0 0.8 fusion.76
  82.8 0.8 fusion.77
  83.6 0.6 bitcast_dynamic-update-slice_fusion.2
  84.2 0.6 dynamic_slice.49
  86.8 0.6 dynamic_slice.48
  89.3 3.6 %multiply_subtract_fusion.3 = (f32[1,1,32,2048]{2,3,1,0:T(8,128)}, f32[1,1,32,2048]{2,3,1,0:T(8,128)S(1)}, f32[1,1,32,2048]{2,3,1,0:T(8,128)S(1)}, f32[1,1,32,2048]{2,3,1,0:T(8,128)S(1)}) fusion(f32[8,2,32,2048]{2,3,1,0:T(8,128)} %get-tuple-element.285, s32[]{:T(128)S(6)} %select_n.77, s32[]{:T(128)S(6)} %select_n.78, s32[]{:T(128)S(6)} %add.343), kind=kLoop, calls=%fused_computation.11.clone.1 | loop fusion | flops 786432 | bytes 2097164 | tf_op jit(solution)/shard_map/while/body/eval_jaxpr/sub | solution.py:49
  92.9 1.7 %copy.35 = f32[1,32,128,16]{2,3,1,0:T(8,128)S(1)} copy(f32[1,32,128,16]{1,3,2,0:T(8,128)} %bitcast.86) | data formatting | bytes 524288 | tf_op jit(solution)/shard_map/while/body/eval_jaxpr/sub | solution.py:49
  94.5 1.2 copy.36
  96.4 0.7 fusion.72
  97.1 0.7 iota_multiply_fusion.2
  98.0 2.1 %multiply_add_fusion.5 = (f32[1,32,128,16]{2,3,1,0:T(8,128)S(1)}, f32[1,32,128,16]{2,3,1,0:T(8,128)S(1)}) fusion(f32[1,32,128,16]{2,3,1,0:T(8,128)S(1)} %copy.35, f32[1,32,128,16]{2,3,1,0:T(8,128)} %copy.36, f32[32]{0:T(128)S(1)} %fusion.72, f32[128,16]{0,1:T(8,128)S(1)} %copy.37), kind=kLoop, calls=%fused_computation.14.clone.1 | loop fusion | flops 524288 | bytes 1056896 | tf_op jit(solution)/shard_map/while/body/eval_jaxpr/add | solution.py:61
  101.1 0.7 fusion.75
  101.9 0.8 fusion.74
  102.7 0.8 fusion.76
  103.5 0.8 fusion.77
  104.3 0.7 bitcast_dynamic-update-slice_fusion.2
  105.0 0.6 dynamic_slice.49
  107.5 0.6 dynamic_slice.48
  110.0 3.6 %multiply_subtract_fusion.3 = (f32[1,1,32,2048]{2,3,1,0:T(8,128)}, f32[1,1,32,2048]{2,3,1,0:T(8,128)S(1)}, f32[1,1,32,2048]{2,3,1,0:T(8,128)S(1)}, f32[1,1,32,2048]{2,3,1,0:T(8,128)S(1)}) fusion(f32[8,2,32,2048]{2,3,1,0:T(8,128)} %get-tuple-element.285, s32[]{:T(128)S(6)} %select_n.77, s32[]{:T(128)S(6)} %select_n.78, s32[]{:T(128)S(6)} %add.343), kind=kLoop, calls=%fused_computation.11.clone.1 | loop fusion | flops 786432 | bytes 2097164 | tf_op jit(solution)/shard_map/while/body/eval_jaxpr/sub | solution.py:49
  113.6 1.7 %copy.35 = f32[1,32,128,16]{2,3,1,0:T(8,128)S(1)} copy(f32[1,32,128,16]{1,3,2,0:T(8,128)} %bitcast.86) | data formatting | bytes 524288 | tf_op jit(solution)/shard_map/while/body/eval_jaxpr/sub | solution.py:49
  115.3 1.2 copy.36
  117.1 0.7 fusion.72
  117.8 0.7 iota_multiply_fusion.2
  118.7 2.1 %multiply_add_fusion.5 = (f32[1,32,128,16]{2,3,1,0:T(8,128)S(1)}, f32[1,32,128,16]{2,3,1,0:T(8,128)S(1)}) fusion(f32[1,32,128,16]{2,3,1,0:T(8,128)S(1)} %copy.35, f32[1,32,128,16]{2,3,1,0:T(8,128)} %copy.36, f32[32]{0:T(128)S(1)} %fusion.72, f32[128,16]{0,1:T(8,128)S(1)} %copy.37), kind=kLoop, calls=%fused_computation.14.clone.1 | loop fusion | flops 524288 | bytes 1056896 | tf_op jit(solution)/shard_map/while/body/eval_jaxpr/add | solution.py:61
  121.8 0.7 fusion.75
  122.6 0.8 fusion.74
  123.4 0.8 fusion.76
  124.2 0.8 fusion.77
  125.1 0.7 bitcast_dynamic-update-slice_fusion.2
  125.7 0.9 fusion.55
  126.6 4.6 %collective-permute-start.1 = (f32[4,4,8,128]{3,2,1,0:T(8,128)S(1)}, f32[4,4,8,128]{3,2,1,0:T(8,128)S(1)}, u32[]{:S(2)}, u32[]{:S(2)}) collective-permute-start(f32[4,4,8,128]{3,2,1,0:T(8,128)S(1)} %get-tuple-element.197), channel_id=1, source_target_pairs={{0,1},{1,2},{2,3},{3,4},{4,5},{5,6},{6,7},{8,9},{9,10},{10,11},{11... | collective-permute-start | bytes 196616 | tf_op jit(solution)/shard_map/ppermute | solution.py:22
  131.2 1.9 %collective-permute-start.2 = (f32[4,4,8,128]{3,2,1,0:T(8,128)S(1)}, f32[4,4,8,128]{3,2,1,0:T(8,128)S(1)}, u32[]{:S(2)}, u32[]{:S(2)}) collective-permute-start(f32[4,4,8,128]{3,2,1,0:T(8,128)S(1)} %get-tuple-element.198), channel_id=1, source_target_pairs={{1,0},{2,1},{3,2},{4,3},{5,4},{6,5},{7,6},{9,8},{10,9},{11,10},{12... | collective-permute-start | bytes 196616 | tf_op jit(solution)/shard_map/ppermute | solution.py:23
  133.2 7.8 %collective-permute-done.2 = f32[4,4,8,128]{3,2,1,0:T(8,128)S(1)} collective-permute-done((f32[4,4,8,128]{3,2,1,0:T(8,128)S(1)}, f32[4,4,8,128]{3,2,1,0:T(8,128)S(1)}, u32[]{:S(2)}, u32[]{:S(2)}) %collective-permute-start.2) | collective-permute-done | bytes 65568 | tf_op jit(solution)/shard_map/ppermute | solution.py:23
  141.0 1.3 convolution_bitcast_fusion
  142.4 0.7 pad_maximum_fusion.3
  (41 shorter events, 7.6 us)
Async XLA Ops:
  0.0 28.5 %collective-permute-start = (f32[4,2,32,2048]{3,2,1,0:T(8,128)}, f32[4,2,32,2048]{3,2,1,0:T(8,128)S(1)}, u32[]{:S(2)}, u32[]{:S(2)}) collective-permute-start(f32[4,2,32,2048]{3,2,1,0:T(8,128)} %param.5), channel_id=1, source_target_pairs={{0,8},{8,16},{16,24},{24,32},{32,40},{40,48},{48,56},{56,64},{64,7... | collective-permute-start | bytes 6291464 | tf_op jit(solution)/shard_map/ppermute | solution.py:12
  32.4 10.4 %copy-start = (s32[4,2]{0,1:T(2,128)S(1)}, s32[4,2]{0,1:T(2,128)}, u32[]{:S(2)}) copy-start(s32[4,2]{0,1:T(2,128)} %param.7) | copy-start | bytes 100
  126.6 6.5 %collective-permute-start.1 = (f32[4,4,8,128]{3,2,1,0:T(8,128)S(1)}, f32[4,4,8,128]{3,2,1,0:T(8,128)S(1)}, u32[]{:S(2)}, u32[]{:S(2)}) collective-permute-start(f32[4,4,8,128]{3,2,1,0:T(8,128)S(1)} %get-tuple-element.197), channel_id=1, source_target_pairs={{0,1},{1,2},{2,3},{3,4},{4,5},{5,6},{6,7},{8,9},{9,10},{10,11},{11... | collective-permute-start | bytes 196616 | tf_op jit(solution)/shard_map/ppermute | solution.py:22
  131.2 9.8 %collective-permute-start.2 = (f32[4,4,8,128]{3,2,1,0:T(8,128)S(1)}, f32[4,4,8,128]{3,2,1,0:T(8,128)S(1)}, u32[]{:S(2)}, u32[]{:S(2)}) collective-permute-start(f32[4,4,8,128]{3,2,1,0:T(8,128)S(1)} %get-tuple-element.198), channel_id=1, source_target_pairs={{1,0},{2,1},{3,2},{4,3},{5,4},{6,5},{7,6},{9,8},{10,9},{11,10},{12... | collective-permute-start | bytes 196616 | tf_op jit(solution)/shard_map/ppermute | solution.py:23
where the time goes:
time: 145 us; the launch traced here: 143 us
  other arithmetic  36.8 us (25%)
  local copies, waits for them, and re-layouts  34.9 us (24%)
  waiting for transfers between devices  33.6 us (23%)
  loops' own time  15.3 us (11%)
  matrix products  13.9 us (10%)
  starting transfers between devices  8.42 us (6%)
    ppermute x1, waiting for transfers between devices, passed_along(): return lax.ppermute(block, axis, route)  25.8 us
    another operation x1, loops' own time, pair_looks(): return lax.map(per_pair, (ref_index, sec_index, phase_ramps))  15.3 us
    sub x4, other arithmetic, interfere(): imag_part = imag_first * real_second - real_first * imag_second  14.4 us
    dot_general x16, matrix products, range_look(): jnp.einsum('flok,k->flo', blocked[:, :, offset:offset + outputs, :], tap_...  12.6 us
    unnamed x3, local copies, waits for them, and re-layouts  10.4 us
    add x4, other arithmetic, interfere(): real_part * cosine + imag_part * sine  8.34 us
    ppermute x1, waiting for transfers between devices, with_halo(): after = lax.ppermute(initial, axis, down)  7.83 us
    sub x4, local copies, waits for them, and re-layouts, interfere(): imag_part = imag_first * real_second - real_first * imag_second  6.68 us
  transfers between devices with their start and end apart: 3, of which 2 were waited for; matrix products, arithmetic and copies ran while one was open for 1% of the time, Pallas kernels for 0%

commit v1 on v0

v1 whole, which is shorter than its diff:
```python
import functools
import math

import jax
import jax.numpy as jnp
from jax import lax
from jax.experimental import pallas as pl
from jax.experimental.pallas import tpu as pltpu
from jax.sharding import PartitionSpec as P

MESH = pl.DeviceIdType.MESH
F32, BF16, I32 = jnp.float32, jnp.bfloat16, jnp.int32
LINES = 8
PARTS = 2
STEP = 16
TILE = 256


def iota(shape, dim):
    return lax.broadcasted_iota(I32, shape, dim)


def split(value):
    high = value.astype(BF16)
    return high, (value - high.astype(F32)).astype(BF16)


def turns(count, whole):
    angle = (count & (whole - 1)).astype(F32) * (2.0 * math.pi / whole)
    return jnp.cos(angle), jnp.sin(angle)


def group_order(groups):
    return [0, groups - 1] + list(range(1, groups - 1))


def kernel(
    sizes, echoes, pairs, ramps, out, pieces, pair_mem, ramp_mem, weights, table, line_table,
    fields, sums, looks, above, below, send_sem, recv_sem, own_sem, small_sem, edge_send, edge_recv,
):
    acqs, groups, width, acq_size, strip_size = sizes
    reach = acqs - 1
    part_width = width // PARTS
    outputs = width // STEP
    lines = groups * LINES
    acq, strip = lax.axis_index("acq"), lax.axis_index("strip")
    has_next, has_previous = acq < acq_size - 1, acq > 0
    has_below, has_above = strip < strip_size - 1, strip > 0
    chunks = [(g, h) for g in group_order(groups) for h in range(PARTS)]

    barrier = pltpu.get_barrier_semaphore()

    def greet(condition, target):
        @pl.when(condition)
        def _():
            pl.semaphore_signal(barrier, inc=1, device_id=target, device_id_type=MESH)

    greet(has_previous, {"acq": acq - 1})
    greet(has_next, {"acq": acq + 1})
    greet(has_above, {"strip": strip - 1})
    greet(has_below, {"strip": strip + 1})

    pair_copy = pltpu.make_async_copy(pairs, pair_mem, small_sem.at[0])
    ramp_copy = pltpu.make_async_copy(ramps, ramp_mem, small_sem.at[1])
    pair_copy.start()
    ramp_copy.start()

    def region(first, g, h):
        return echoes.at[
            pl.ds(first, acqs - first), :, pl.ds(g * LINES, LINES), pl.ds(h * part_width, part_width)
        ]

    own, sent = [], []
    for i, (g, h) in enumerate(chunks):
        own.append(
            pltpu.make_async_copy(
                region(0, g, h), pieces[i].at[pl.ds(reach, acqs)], own_sem.at[i]
            )
        )
        sent.append(
            pltpu.make_async_remote_copy(
                region(1, g, h), pieces[i].at[pl.ds(0, reach)], send_sem.at[i], recv_sem.at[i],
                device_id={"acq": acq + 1}, device_id_type=MESH,
            )
        )

    neighbours = sum(c.astype(I32) for c in (has_next, has_previous, has_below, has_above))
    pl.semaphore_wait(barrier, neighbours)

    @pl.when(has_next)
    def _():
        for copy in sent:
            copy.start()

    for copy in own:
        copy.start()

    @pl.loop(0, width // TILE)
    def _(t):
        rows = pl.ds(pl.multiple_of(t * TILE, TILE), TILE)
        offset = iota((TILE, outputs), 0) + t * TILE - STEP * iota((TILE, outputs), 1)
        shifted = offset.astype(F32) + 0.5
        taps = jnp.exp(-(shifted * shifted) / 512.0)
        high, low = split(jnp.where((offset >= -32) & (offset < 32), taps, 0.0))
        weights[rows, 0:outputs] = high
        weights[rows, outputs : 2 * outputs] = low

    pair_copy.wait()
    ramp_copy.wait()

    @pl.loop(0, acqs)
    def _(p):
        cosine, sine = turns(ramp_mem[p, 0] * iota((LINES, width), 1), width)
        table[p, 0] = cosine
        table[p, 1] = sine
        line = strip * lines + iota((lines, outputs), 0)
        cosine, sine = turns(ramp_mem[p, 1] * line, lines * strip_size)
        line_table[p, 0] = cosine
        line_table[p, 1] = sine

    @pl.when(jnp.logical_not(has_above))
    def _():
        above[...] = jnp.zeros_like(above)

    @pl.when(jnp.logical_not(has_below))
    def _():
        below[...] = jnp.zeros_like(below)

    slots = [jnp.clip(pair_mem[p, 0] - acq * acqs + reach, 0, reach + acqs - 1) for p in range(acqs)]
    half = acqs * 4 * LINES
    edge_up = pltpu.make_async_remote_copy(
        looks[0], below, edge_send.at[0], edge_recv.at[0],
        device_id={"strip": strip - 1}, device_id_type=MESH,
    )
    edge_down = pltpu.make_async_remote_copy(
        looks[groups - 1], above, edge_send.at[1], edge_recv.at[1],
        device_id={"strip": strip + 1}, device_id_type=MESH,
    )

    for i, (g, h) in enumerate(chunks):
        own[i].wait()

        @pl.when(has_previous)
        def _():
            sent[i].wait_recv()

        piece = pieces[i]
        for t in range(part_width // TILE):
            here = pl.ds(t * TILE, TILE)
            there = pl.ds(h * part_width + t * TILE, TILE)
            for p in range(acqs):
                a, b = piece[slots[p], 0, :, here], piece[slots[p], 1, :, here]
                c, d = piece[reach + p, 0, :, here], piece[reach + p, 1, :, here]
                cosine, sine = table[p, 0, :, there], table[p, 1, :, there]
                x, y = a * c + b * d, b * c - a * d
                value = jnp.concatenate(
                    [x * cosine + y * sine, y * cosine - x * sine, a * a + b * b, c * c + d * d]
                )
                high, low = split(value)
                fields[pl.ds(p * 4 * LINES, 4 * LINES), here] = high
                fields[pl.ds(half + p * 4 * LINES, 4 * LINES), here] = low
        product = jnp.dot(
            fields[...], weights[pl.ds(h * part_width, part_width), :], preferred_element_type=F32
        )
        part = (
            product[:half, :outputs] + product[:half, outputs:] + product[half:, :outputs]
        )
        if h == 0:
            sums[...] = part
        elif h < PARTS - 1:
            sums[...] += part
        if h == PARTS - 1:
            whole = sums[...] + part if PARTS > 1 else part
            whole = whole.reshape(acqs, 4, LINES, outputs)
            for p in range(acqs):
                now = pl.ds(g * LINES, LINES)
                cosine, sine = line_table[p, 0, now, :], line_table[p, 1, now, :]
                x, y = whole[p, 0], whole[p, 1]
                looks[g][p, 0] = x * cosine + y * sine
                looks[g][p, 1] = y * cosine - x * sine
                looks[g][p, 2] = whole[p, 2]
                looks[g][p, 3] = whole[p, 3]
            if g == 0:

                @pl.when(has_above)
                def _():
                    edge_up.start()

            if g == groups - 1:

                @pl.when(has_below)
                def _():
                    edge_down.start()

    @pl.when(has_above)
    def _():
        edge_down.wait_recv()

    @pl.when(has_below)
    def _():
        edge_up.wait_recv()

    offset = iota((lines, lines + 2 * LINES), 1) - iota((lines, lines + 2 * LINES), 0) - LINES
    value = offset.astype(F32)
    band = jnp.where(
        (offset >= -LINES) & (offset <= LINES), jnp.exp(-(value * value) / 32.0), 0.0
    )
    high, low = split(band)
    band = jnp.concatenate([high, high, low], axis=1)
    for p in range(acqs):
        summed = []
        for k in range(0, 4, 2):
            value = jnp.concatenate(
                [
                    jnp.concatenate([source[p, k], source[p, k + 1]], axis=1)
                    for source in (above, *looks, below)
                ]
            )
            high, low = split(value)
            value = jnp.concatenate([high, low, high])
            value = jnp.dot(band, value, preferred_element_type=F32)
            summed += [value[:, :outputs], value[:, outputs:]]
        scaling = 1.0 / jnp.sqrt(summed[2] * summed[3] + 1e-06)
        out[p, 0] = summed[0] * scaling
        out[p, 1] = summed[1] * scaling

    @pl.when(has_next)
    def _():
        for copy in sent:
            copy.wait_send()

    @pl.when(has_above)
    def _():
        edge_up.wait_send()

    @pl.when(has_below)
    def _():
        edge_down.wait_send()


def body(echoes, pair_list, phase_ramps):
    acqs, _, lines, width = echoes.shape
    groups = lines // LINES
    outputs = width // STEP
    chunks = groups * PARTS
    sizes = (acqs, groups, width, lax.axis_size("acq"), lax.axis_size("strip"))
    dma = pltpu.SemaphoreType.DMA
    look = pltpu.VMEM((acqs, 4, LINES, outputs), F32)
    return pl.pallas_call(
        functools.partial(kernel, sizes),
        out_shape=jax.ShapeDtypeStruct((acqs, 2, lines, outputs), F32),
        in_specs=[pl.BlockSpec(memory_space=pl.ANY)] * 3,
        out_specs=pl.BlockSpec(memory_space=pltpu.VMEM),
        scratch_shapes=[
            [pltpu.VMEM((2 * acqs - 1, 2, LINES, width // PARTS), F32) for _ in range(chunks)],
            pltpu.SMEM(pair_list.shape, I32),
            pltpu.SMEM(phase_ramps.shape, I32),
            pltpu.VMEM((width, 2 * outputs), BF16),
            pltpu.VMEM((acqs, 2, LINES, width), F32),
            pltpu.VMEM((acqs, 2, lines, outputs), F32),
            pltpu.VMEM((2 * acqs * 4 * LINES, width // PARTS), BF16),
            pltpu.VMEM((acqs * 4 * LINES, outputs), F32),
            [look for _ in range(groups)],
            look,
            look,
            dma((chunks,)),
            dma((chunks,)),
            dma((chunks,)),
            dma((2,)),
            dma((2,)),
            dma((2,)),
        ],
        compiler_params=pltpu.CompilerParams(collective_id=0, has_side_effects=True),
    )(echoes, pair_list, phase_ramps)


def solution(mesh):
    return jax.shard_map(
        body,
        mesh=mesh,
        in_specs=(P("acq", None, "strip", None), P("acq", None), P("acq", None)),
        out_specs=P("acq", None, "strip", None),
        check_vma=False,
    )
```

time: 145 us -> 31.7 us (0.22)
  the two profiles are of different devices: /device:TPU:184 before, /device:TPU:135 now
where the time goes in v1:
time: 31.7 us; the launch traced here: 31.6 us
  Pallas kernels  27.3 us (86%)
  local copies, waits for them, and re-layouts  4.25 us (13%)
    pallas_call x1, Pallas kernels, body(): pl.pallas_call(functools.partial(kernel, sizes), out_shape=jax.ShapeDtype...  27.3 us
    unnamed x3, local copies, waits for them, and re-layouts  4.25 us

profile of v1, /device:TPU:135, one launch (start us, length us, event | category | flops | bytes accessed | tf_op | source)
XLA Modules:
  0.0 31.6 jit_solution(4841005323373625588)
XLA Ops:
  0.0 1.3 %copy.4.pairs = s32[4,2]{1,0:T(4,128)} copy(s32[4,2]{0,1:T(2,128)} %param.4) | data formatting | bytes 64 | tf_op args[1]
  1.3 1.3 %copy.5.ramps = s32[4,2]{1,0:T(4,128)} copy(s32[4,2]{0,1:T(2,128)} %param.5) | data formatting | bytes 64 | tf_op args[2]
  2.7 27.3 %shard_map.37 = f32[4,2,32,128]{3,2,1,0:T(8,128)} custom-call(f32[4,2,32,2048]{3,2,1,0:T(8,128)} %echoes.1, s32[4,2]{1,0:T(4,128)} %copy.4.pairs, s32[4,2]{1,0:T(4,128)} %copy.5.ramps), custom_call_target="tpu_custom_call" | custom-call | tf_op jit(solution)/shard_map/pallas_call | solution.py:249
  30.0 1.6 %copy.7 = f32[4,2,32,128]{3,2,1,0:T(8,128)} copy(f32[4,2,32,128]{3,2,1,0:T(8,128)} %shard_map.37) | data formatting | bytes 262144

commit v2 on v1

v2 whole, which is shorter than its diff:
```python
import functools
import math

import jax
import jax.numpy as jnp
from jax import lax
from jax.experimental import pallas as pl
from jax.experimental.pallas import tpu as pltpu
from jax.sharding import PartitionSpec as P

MESH = pl.DeviceIdType.MESH
F32, BF16, I32 = jnp.float32, jnp.bfloat16, jnp.int32
LINES = 8
PARTS = (1024, 1024)
LAST_PARTS = (1024, 768, 256)
DEPTH = 3
RELAY_AT = 4
CHIPS = 4
STEP = 16
TILE = 256


def iota(shape, dim):
    return lax.broadcasted_iota(I32, shape, dim)


def split(value):
    high = value.astype(BF16)
    return high, (value - high.astype(F32)).astype(BF16)


def turns(count, whole):
    angle = (count & (whole - 1)).astype(F32) * (2.0 * math.pi / whole)
    return jnp.cos(angle), jnp.sin(angle)


def group_order(groups):
    return [0, groups - 1] + list(range(1, groups - 1))


def chunk_list(groups):
    chunks = []
    for g in group_order(groups):
        parts = LAST_PARTS if g == group_order(groups)[-1] else PARTS
        start = 0
        for i, count in enumerate(parts):
            chunks.append((g, start, count, i == 0, i == len(parts) - 1))
            start += count
    return chunks


def kernel(
    sizes, echoes, pairs, ramps, out, pieces, pair_mem, ramp_mem, weights, table, line_table,
    fields, sums, partial, looks, above, below, relayed, send_sem, recv_sem, own_sem, small_sem, edge_send, edge_recv,
    relay_send, relay_recv,
):
    acqs, groups, width, acq_size, strip_size = sizes
    reach = acqs - 1
    outputs = width // STEP
    lines = groups * LINES
    acq, strip = lax.axis_index("acq"), lax.axis_index("strip")
    has_next, has_previous = acq < acq_size - 1, acq > 0
    has_below, has_above = strip < strip_size - 1, strip > 0
    place = lax.rem(acq, CHIPS)
    middle = strip_size // 2
    on_second = place >= CHIPS // 2
    relay_down, relay_up = on_second & (strip == middle - 1), on_second & (strip == middle)
    direct_down = has_below & jnp.logical_not(relay_down)
    direct_up = has_above & jnp.logical_not(relay_up)
    relays_up, relays_down = (place == 0) & (strip == 0), (place == 0) & (strip == strip_size - 1)
    first_strip, last_strip = jnp.int32(0), jnp.int32(strip_size - 1)
    chunks = chunk_list(groups)
    last_group = group_order(groups)[-1]

    barrier = pltpu.get_barrier_semaphore()

    def greet(condition, target):
        @pl.when(condition)
        def _():
            pl.semaphore_signal(barrier, inc=1, device_id=target, device_id_type=MESH)

    greet(has_previous, {"acq": acq - 1})
    greet(has_above & jnp.logical_not(relay_up), {"strip": strip - 1})
    greet(has_below & jnp.logical_not(relay_down), {"strip": strip + 1})
    greet(relay_up, {"acq": acq - place, "strip": last_strip})
    greet(relay_down, {"acq": acq - place, "strip": first_strip})
    for j in range(2):
        greet(relays_up, {"acq": acq + CHIPS // 2 + j, "strip": jnp.int32(middle)})
        greet(relays_down, {"acq": acq + CHIPS // 2 + j, "strip": jnp.int32(middle - 1)})

    pair_copy = pltpu.make_async_copy(pairs, pair_mem, small_sem.at[0])
    ramp_copy = pltpu.make_async_copy(ramps, ramp_mem, small_sem.at[1])
    pair_copy.start()
    ramp_copy.start()

    def region(first, g, start, count):
        return echoes.at[
            pl.ds(first, acqs - first), :, pl.ds(g * LINES, LINES), pl.ds(start, count)
        ]

    own, sent = [], []
    for i, (g, start, count, _, _) in enumerate(chunks):
        own.append(
            pltpu.make_async_copy(
                region(0, g, start, count), pieces[i].at[pl.ds(reach, acqs)], own_sem.at[i]
            )
        )
        sent.append(
            pltpu.make_async_remote_copy(
                region(1, g, start, count), pieces[i].at[pl.ds(0, reach)], send_sem.at[i], recv_sem.at[i],
                device_id={"acq": acq + 1}, device_id_type=MESH,
            )
        )

    targets = (has_next, direct_down, direct_up, relay_down, relay_up)
    targets += (relays_up, relays_down, relays_up, relays_down)
    neighbours = sum(c.astype(I32) for c in targets)
    pl.semaphore_wait(barrier, neighbours)

    @pl.when(has_next)
    def _():
        for copy in sent[:DEPTH]:
            copy.start()

    for copy in own:
        copy.start()

    @pl.loop(0, width // TILE)
    def _(t):
        rows = pl.ds(pl.multiple_of(t * TILE, TILE), TILE)
        offset = iota((TILE, outputs), 0) + t * TILE - STEP * iota((TILE, outputs), 1)
        shifted = offset.astype(F32) + 0.5
        taps = jnp.exp(-(shifted * shifted) / 512.0)
        high, low = split(jnp.where((offset >= -32) & (offset < 32), taps, 0.0))
        weights[rows, 0:outputs] = high
        weights[rows, outputs : 2 * outputs] = low

    pair_copy.wait()
    ramp_copy.wait()

    @pl.loop(0, acqs)
    def _(p):
        cosine, sine = turns(ramp_mem[0, p] * iota((LINES, width), 1), width)
        table[p, 0] = cosine
        table[p, 1] = sine
        line = strip * lines + iota((lines, outputs), 0)
        cosine, sine = turns(ramp_mem[1, p] * line, lines * strip_size)
        line_table[p, 0] = cosine
        line_table[p, 1] = sine

    @pl.when(jnp.logical_not(has_above))
    def _():
        above[...] = jnp.zeros_like(above)

    @pl.when(jnp.logical_not(has_below))
    def _():
        below[...] = jnp.zeros_like(below)

    slots = [jnp.clip(pair_mem[0, p] - acq * acqs + reach, 0, reach + acqs - 1) for p in range(acqs)]
    half = acqs * 4 * LINES
    edge_up = pltpu.make_async_remote_copy(
        looks[0], below, edge_send.at[0], edge_recv.at[0],
        device_id={"strip": strip - 1}, device_id_type=MESH,
    )
    edge_down = pltpu.make_async_remote_copy(
        looks[groups - 1], above, edge_send.at[1], edge_recv.at[1],
        device_id={"strip": strip + 1}, device_id_type=MESH,
    )

    offset = iota((lines, lines + 2 * LINES), 1) - iota((lines, lines + 2 * LINES), 0) - LINES
    value = offset.astype(F32)
    taps = jnp.where((offset >= -LINES) & (offset <= LINES), jnp.exp(-(value * value) / 32.0), 0.0)
    taps_high = taps.astype(BF16).astype(F32)
    taps_low = taps - taps_high

    def azimuth(p, k, blocks):
        value = jnp.concatenate(
            [
                jnp.concatenate([source[p, k], source[p, k + 1]], axis=1)
                for _, source in blocks
            ]
        )
        high = value.astype(BF16).astype(F32)
        columns = [
            jnp.concatenate([part[:, j * LINES : (j + 1) * LINES] for j, _ in blocks], axis=1)
            for part in (taps_high, taps_low)
        ]
        left = jnp.concatenate([columns[0], columns[0], columns[1]], axis=1)
        right = jnp.concatenate([high, value - high, high])
        return jnp.dot(left.astype(BF16), right.astype(BF16), preferred_element_type=F32)

    lane = jnp.maximum(place - CHIPS // 2, 0)

    def to_relay(source, target):
        return pltpu.make_async_remote_copy(
            source, relayed.at[lane], edge_send.at[2], relay_recv.at[lane],
            device_id={"acq": acq - place, "strip": target}, device_id_type=MESH,
        )

    to_relay_up = to_relay(looks[0], first_strip)
    to_relay_down = to_relay(looks[groups - 1], last_strip)

    def from_relay(j, target, room, recv):
        return pltpu.make_async_remote_copy(
            relayed.at[j], room, relay_send.at[j], edge_recv.at[recv],
            device_id={"acq": acq + CHIPS // 2 + j, "strip": jnp.int32(target)}, device_id_type=MESH,
        )

    from_relay_up = [from_relay(j, middle - 1, below, 0) for j in range(2)]
    from_relay_down = [from_relay(j, middle, above, 1) for j in range(2)]
    from_second = [
        pltpu.make_async_remote_copy(
            relayed.at[j], relayed.at[j], relay_send.at[j], relay_recv.at[j],
            device_id={"acq": acq}, device_id_type=MESH,
        )
        for j in range(2)
    ]

    for i, (g, start, count, first_part, last_part) in enumerate(chunks):
        if i == RELAY_AT:
            for condition, copies in ((relays_up, from_relay_up), (relays_down, from_relay_down)):

                @pl.when(condition)
                def _():
                    for j, copy in enumerate(copies):
                        from_second[j].wait_recv()
                        copy.start()

        if i + DEPTH < len(chunks):

            @pl.when(has_next)
            def _():
                sent[i].wait_send()
                sent[i + DEPTH].start()

        if i == len(chunks) - 1:

            @pl.when(has_above)
            def _():
                edge_down.wait_recv()

            @pl.when(has_below)
            def _():
                edge_up.wait_recv()

            blocks = [(0, above), (groups + 1, below)]
            blocks += [(j + 1, looks[j]) for j in range(groups) if j != last_group]
            for p in range(acqs):
                for k in range(0, 4, 2):
                    partial[p, k // 2] = azimuth(p, k, blocks)

        own[i].wait()

        @pl.when(has_previous)
        def _():
            sent[i].wait_recv()

        piece = pieces[i]
        for t in range(count // TILE):
            here = pl.ds(t * TILE, TILE)
            there = pl.ds(start + t * TILE, TILE)
            for p in range(acqs):
                a, b = piece[slots[p], 0, :, here], piece[slots[p], 1, :, here]
                c, d = piece[reach + p, 0, :, here], piece[reach + p, 1, :, here]
                cosine, sine = table[p, 0, :, there], table[p, 1, :, there]
                x, y = a * c + b * d, b * c - a * d
                value = jnp.concatenate(
                    [x * cosine + y * sine, y * cosine - x * sine, a * a + b * b, c * c + d * d]
                )
                high, low = split(value)
                fields[pl.ds(p * 4 * LINES, 4 * LINES), here] = high
                fields[pl.ds(half + p * 4 * LINES, 4 * LINES), here] = low
        product = jnp.dot(
            fields[:, 0:count], weights[pl.ds(start, count), :], preferred_element_type=F32
        )
        part = (
            product[:half, :outputs] + product[:half, outputs:] + product[half:, :outputs]
        )
        if first_part:
            sums[...] = part
        elif not last_part:
            sums[...] += part
        if last_part:
            whole = part if first_part else sums[...] + part
            whole = whole.reshape(acqs, 4, LINES, outputs)
            for p in range(acqs):
                now = pl.ds(g * LINES, LINES)
                cosine, sine = line_table[p, 0, now, :], line_table[p, 1, now, :]
                x, y = whole[p, 0], whole[p, 1]
                looks[g][p, 0] = x * cosine + y * sine
                looks[g][p, 1] = y * cosine - x * sine
                looks[g][p, 2] = whole[p, 2]
                looks[g][p, 3] = whole[p, 3]
            if g == 0:

                @pl.when(direct_up)
                def _():
                    edge_up.start()

                @pl.when(relay_up)
                def _():
                    to_relay_up.start()

            if g == groups - 1:

                @pl.when(direct_down)
                def _():
                    edge_down.start()

                @pl.when(relay_down)
                def _():
                    to_relay_down.start()

    for p in range(acqs):
        summed = []
        for k in range(0, 4, 2):
            value = partial[p, k // 2] + azimuth(p, k, [(last_group + 1, looks[last_group])])
            summed += [value[:, :outputs], value[:, outputs:]]
        scaling = 1.0 / jnp.sqrt(summed[2] * summed[3] + 1e-06)
        out[p, 0] = summed[0] * scaling
        out[p, 1] = summed[1] * scaling

    @pl.when(has_next)
    def _():
        for copy in sent[-DEPTH:]:
            copy.wait_send()

    for condition, copies in (
        (direct_up, [edge_up]),
        (direct_down, [edge_down]),
        (relay_up, [to_relay_up]),
        (relay_down, [to_relay_down]),
        (relays_up, from_relay_up),
        (relays_down, from_relay_down),
    ):

        @pl.when(condition)
        def _():
            for copy in copies:
                copy.wait_send()


def body(echoes, pair_list, phase_ramps):
    acqs, _, lines, width = echoes.shape
    groups = lines // LINES
    outputs = width // STEP
    chunks = chunk_list(groups)
    sizes = (acqs, groups, width, lax.axis_size("acq"), lax.axis_size("strip"))
    dma = pltpu.SemaphoreType.DMA
    look = pltpu.VMEM((acqs, 4, LINES, outputs), F32)
    return pl.pallas_call(
        functools.partial(kernel, sizes),
        out_shape=jax.ShapeDtypeStruct((acqs, 2, lines, outputs), F32),
        in_specs=[pl.BlockSpec(memory_space=pl.ANY)] * 3,
        out_specs=pl.BlockSpec(memory_space=pltpu.VMEM),
        scratch_shapes=[
            [pltpu.VMEM((2 * acqs - 1, 2, LINES, c[2]), F32) for c in chunks],
            pltpu.SMEM((2, acqs), I32),
            pltpu.SMEM((2, acqs), I32),
            pltpu.VMEM((width, 2 * outputs), BF16),
            pltpu.VMEM((acqs, 2, LINES, width), F32),
            pltpu.VMEM((acqs, 2, lines, outputs), F32),
            pltpu.VMEM((2 * acqs * 4 * LINES, max(c[2] for c in chunks)), BF16),
            pltpu.VMEM((acqs * 4 * LINES, outputs), F32),
            pltpu.VMEM((acqs, 2, lines, 2 * outputs), F32),
            [look for _ in range(groups)],
            look,
            look,
            pltpu.VMEM((2, acqs, 4, LINES, outputs), F32),
            dma((len(chunks),)),
            dma((len(chunks),)),
            dma((len(chunks),)),
            dma((2,)),
            dma((3,)),
            dma((2,)),
            dma((2,)),
            dma((2,)),
        ],
        compiler_params=pltpu.CompilerParams(collective_id=0, has_side_effects=True, vmem_limit_bytes=16 << 20),
    )(*(pltpu.with_memory_space_constraint(v, pltpu.HBM) for v in (echoes, pair_list.T, phase_ramps.T)))


def solution(mesh):
    return jax.shard_map(
        body,
        mesh=mesh,
        in_specs=(P("acq", None, "strip", None), P("acq", None), P("acq", None)),
        out_specs=P("acq", None, "strip", None),
        check_vma=False,
    )
```

time: 31.7 us -> 25.6 us (0.81)
  the two profiles are of different devices: /device:TPU:135 before, /device:TPU:103 now
where the time goes in v2:
time: 25.6 us
  Pallas kernels  24.9 us (97%)
  local copies, waits for them, and re-layouts  0.66 us (3%)
    pallas_call x1, Pallas kernels, body(): pl.pallas_call(functools.partial(kernel, sizes), out_shape=jax.ShapeDtype...  24.9 us
    unnamed x1, local copies, waits for them, and re-layouts  0.66 us

profile of v2, /device:TPU:103, one launch (start us, length us, event | category | flops | bytes accessed | tf_op | source)
XLA Modules:
  0.0 25.6 jit_solution(2858562096590848878)
XLA Ops:
  0.0 24.9 %shard_map.37 = f32[4,2,32,128]{3,2,1,0:T(8,128)S(1)} custom-call(f32[4,2,32,2048]{3,2,1,0:T(8,128)} %echoes.1, s32[2,4]{1,0:T(2,128)} %bitcast.2, s32[2,4]{1,0:T(2,128)} %bitcast.3), custom_call_target="tpu_custom_call" | custom-call | tf_op jit(solution)/shard_map/pallas_call | solution.py:351
  24.9 0.7 %copy.5 = f32[4,2,32,128]{3,2,1,0:T(8,128)} copy(f32[4,2,32,128]{3,2,1,0:T(8,128)S(1)} %shard_map.37) | data formatting | bytes 262144

commit v3 on v2

v3 whole, which is shorter than its diff:
```python
import functools
import math

import jax
import jax.numpy as jnp
from jax import lax
from jax.experimental import pallas as pl
from jax.experimental.pallas import tpu as pltpu
from jax.sharding import PartitionSpec as P

MESH = pl.DeviceIdType.MESH
F32, BF16, I32 = jnp.float32, jnp.bfloat16, jnp.int32
LINES = 8
PARTS = (1024, 1024)
LAST_PARTS = (1024, 768, 256)
DEPTH = 3
RELAY_AT = 3
CHIPS = 4
STEP = 16
TILE = 256


def iota(shape, dim):
    return lax.broadcasted_iota(I32, shape, dim)


def split(value):
    high = value.astype(BF16)
    return high, (value - high.astype(F32)).astype(BF16)


def turns(count, whole):
    angle = (count & (whole - 1)).astype(F32) * (2.0 * math.pi / whole)
    return jnp.cos(angle), jnp.sin(angle)


def chunk_list(groups):
    chunks = []
    for g in range(groups):
        parts = LAST_PARTS if g == groups - 1 else PARTS
        start = 0
        for i, count in enumerate(parts):
            chunks.append((g, start, count, i == 0, i == len(parts) - 1))
            start += count
    return chunks


def kernel(
    sizes, echoes, pairs, ramps, out, pieces, pair_mem, ramp_mem, weights, table, line_table, fields,
    sums, partial, looks, edges, relayed, send_sem, recv_sem, own_sem, small_sem, edge_send, edge_recv,
    relay_recv,
):
    acqs, groups, width, acq_size, strip_size = sizes
    reach = acqs - 1
    outputs = width // STEP
    lines = groups * LINES
    acq, strip = lax.axis_index("acq"), lax.axis_index("strip")
    has_next, has_previous = acq < acq_size - 1, acq > 0
    place = lax.rem(acq, CHIPS)
    middle, last = strip_size // 2, strip_size - 1

    upper = strip < middle
    inner = jnp.where(upper, strip + 1, strip - 1)
    outer = jnp.where(upper, strip - 1, strip + 1)
    outer_room = jnp.where(upper, 0, 1)
    inner_room = 1 - outer_room
    has_outer = (strip > 0) & (strip < last)
    order = [jnp.where(upper, groups - 1, 0), jnp.where(upper, 0, groups - 1), *range(1, groups - 1)]
    first_line = [pl.multiple_of(g * LINES, LINES) for g in order]

    crosses = ((strip == middle - 1) | (strip == middle)) & (place != 0)
    down_relay = jnp.where(place == 1, middle - 2, jnp.where(place == 2, last, last - 1))
    relay_out = jnp.where(upper, down_relay, last - down_relay)
    relay_in = last - relay_out
    depth = jnp.where(upper, strip, last - strip)
    relays = (place == 0) & (depth < middle - 1)
    from_place = jnp.where(depth == middle - 2, 1, jnp.where(depth == 0, 2, 3))
    relays_down = upper == (from_place == 1)
    relay_from = jnp.where(relays_down, middle - 1, middle)
    relay_to = jnp.where(relays_down, middle, middle - 1)
    relay_room = jnp.where(relays_down, 0, 1)
    chunks = chunk_list(groups)

    barrier = pltpu.get_barrier_semaphore()

    def greet(condition, target):
        @pl.when(condition)
        def _():
            pl.semaphore_signal(barrier, inc=1, device_id=target, device_id_type=MESH)

    greet(has_previous, {"acq": acq - 1})
    greet(jnp.logical_not(crosses), {"strip": inner})
    greet(crosses, {"acq": acq - place, "strip": relay_in})
    greet(has_outer, {"strip": outer})
    greet(relays, {"acq": acq + from_place, "strip": relay_from})

    pair_copy = pltpu.make_async_copy(pairs, pair_mem, small_sem.at[0])
    ramp_copy = pltpu.make_async_copy(ramps, ramp_mem, small_sem.at[1])
    pair_copy.start()
    ramp_copy.start()

    def region(first, g, start, count):
        return echoes.at[
            pl.ds(first, acqs - first), :, pl.ds(first_line[g], LINES), pl.ds(start, count)
        ]

    own, sent = [], []
    for i, (g, start, count, _, _) in enumerate(chunks):
        own.append(
            pltpu.make_async_copy(
                region(0, g, start, count), pieces[i].at[pl.ds(reach, acqs)], own_sem.at[i]
            )
        )
        sent.append(
            pltpu.make_async_remote_copy(
                region(1, g, start, count), pieces[i].at[pl.ds(0, reach)], send_sem.at[i], recv_sem.at[i],
                device_id={"acq": acq + 1}, device_id_type=MESH,
            )
        )

    neighbours = 1 + sum(c.astype(I32) for c in (has_next, has_outer, relays))
    pl.semaphore_wait(barrier, neighbours)

    @pl.when(has_next)
    def _():
        for copy in sent[:DEPTH]:
            copy.start()

    for copy in own:
        copy.start()

    @pl.loop(0, width // TILE)
    def _(t):
        rows = pl.ds(pl.multiple_of(t * TILE, TILE), TILE)
        offset = iota((TILE, outputs), 0) + t * TILE - STEP * iota((TILE, outputs), 1)
        shifted = offset.astype(F32) + 0.5
        taps = jnp.exp(-(shifted * shifted) / 512.0)
        high, low = split(jnp.where((offset >= -32) & (offset < 32), taps, 0.0))
        weights[rows, 0:outputs] = high
        weights[rows, outputs : 2 * outputs] = low

    pair_copy.wait()
    ramp_copy.wait()

    @pl.loop(0, acqs)
    def _(p):
        cosine, sine = turns(ramp_mem[0, p] * iota((LINES, width), 1), width)
        table[p, 0] = cosine
        table[p, 1] = sine
        line = strip * lines + iota((lines, outputs), 0)
        cosine, sine = turns(ramp_mem[1, p] * line, lines * strip_size)
        line_table[p, 0] = cosine
        line_table[p, 1] = sine

    @pl.when(jnp.logical_not(has_outer))
    def _():
        edges[outer_room] = jnp.zeros(edges.shape[1:], F32)

    slots = [jnp.clip(pair_mem[0, p] - acq * acqs + reach, 0, reach + acqs - 1) for p in range(acqs)]
    half = acqs * 4 * LINES

    def edge_copy(source, room, send, recv, target):
        return pltpu.make_async_remote_copy(
            source, room, edge_send.at[send], recv, device_id=target, device_id_type=MESH
        )

    to_inner = edge_copy(
        looks[0], edges.at[outer_room], 0, edge_recv.at[outer_room], {"strip": inner}
    )
    to_outer = edge_copy(
        looks[1], edges.at[inner_room], 1, edge_recv.at[inner_room], {"strip": outer}
    )
    to_relay = edge_copy(
        looks[0], relayed, 0, relay_recv.at[0], {"acq": acq - place, "strip": relay_out}
    )
    from_relay = edge_copy(
        relayed, edges.at[relay_room], 2, edge_recv.at[relay_room],
        {"acq": acq + from_place, "strip": relay_to},
    )

    def tap_columns(first):
        offset = first + iota((lines, LINES), 1) - iota((lines, LINES), 0)
        value = offset.astype(F32)
        inside = (offset >= -LINES) & (offset <= LINES)
        return jnp.where(inside, jnp.exp(-(value * value) / 32.0), 0.0)

    def azimuth(p, k, blocks, left):
        value = jnp.concatenate(
            [jnp.concatenate([block[p, k], block[p, k + 1]], axis=1) for block in blocks]
        )
        high = value.astype(BF16).astype(F32)
        right = jnp.concatenate([high, value - high, high])
        return jnp.dot(left, right.astype(BF16), preferred_element_type=F32)

    def azimuth_left(firsts):
        taps = jnp.concatenate([tap_columns(first) for first in firsts], axis=1)
        high = taps.astype(BF16).astype(F32)
        return jnp.concatenate([high, high, taps - high], axis=1).astype(BF16)

    early_left = azimuth_left([-LINES, lines, *first_line[:-1]])
    late_left = azimuth_left(first_line[-1:])

    for i, (g, start, count, first_part, last_part) in enumerate(chunks):
        if i == RELAY_AT:

            @pl.when(relays)
            def _():
                to_relay.wait_recv()
                from_relay.start()

        if i + DEPTH < len(chunks):

            @pl.when(has_next)
            def _():
                sent[i].wait_send()
                sent[i + DEPTH].start()

        if i == len(chunks) - 2:
            edge_copy(
                looks[0], edges.at[inner_room], 0, edge_recv.at[inner_room], {"strip": inner}
            ).wait_recv()

            @pl.when(has_outer)
            def _():
                to_inner.wait_recv()

            blocks = [edges.at[0], edges.at[1], *looks[:-1]]
            for p in range(acqs):
                for k in range(0, 4, 2):
                    partial[p, k // 2] = azimuth(p, k, blocks, early_left)

        own[i].wait()

        @pl.when(has_previous)
        def _():
            sent[i].wait_recv()

        piece = pieces[i]
        for t in range(count // TILE):
            here = pl.ds(t * TILE, TILE)
            there = pl.ds(start + t * TILE, TILE)
            for p in range(acqs):
                a, b = piece[slots[p], 0, :, here], piece[slots[p], 1, :, here]
                c, d = piece[reach + p, 0, :, here], piece[reach + p, 1, :, here]
                cosine, sine = table[p, 0, :, there], table[p, 1, :, there]
                x, y = a * c + b * d, b * c - a * d
                value = jnp.concatenate(
                    [x * cosine + y * sine, y * cosine - x * sine, a * a + b * b, c * c + d * d]
                )
                high, low = split(value)
                fields[pl.ds(p * 4 * LINES, 4 * LINES), here] = high
                fields[pl.ds(half + p * 4 * LINES, 4 * LINES), here] = low
        product = jnp.dot(
            fields[:, 0:count], weights[pl.ds(start, count), :], preferred_element_type=F32
        )
        part = (
            product[:half, :outputs] + product[:half, outputs:] + product[half:, :outputs]
        )
        if first_part:
            sums[...] = part
        elif not last_part:
            sums[...] += part
        if last_part:
            whole = part if first_part else sums[...] + part
            whole = whole.reshape(acqs, 4, LINES, outputs)
            for p in range(acqs):
                now = pl.ds(first_line[g], LINES)
                cosine, sine = line_table[p, 0, now, :], line_table[p, 1, now, :]
                x, y = whole[p, 0], whole[p, 1]
                looks[g][p, 0] = x * cosine + y * sine
                looks[g][p, 1] = y * cosine - x * sine
                looks[g][p, 2] = whole[p, 2]
                looks[g][p, 3] = whole[p, 3]
            if g == 0:

                @pl.when(crosses)
                def _():
                    to_relay.start()

                @pl.when(jnp.logical_not(crosses))
                def _():
                    to_inner.start()

            if g == 1:

                @pl.when(has_outer)
                def _():
                    to_outer.start()

    for p in range(acqs):
        summed = []
        for k in range(0, 4, 2):
            value = partial[p, k // 2] + azimuth(p, k, looks[-1:], late_left)
            summed += [value[:, :outputs], value[:, outputs:]]
        scaling = 1.0 / jnp.sqrt(summed[2] * summed[3] + 1e-06)
        out[p, 0] = summed[0] * scaling
        out[p, 1] = summed[1] * scaling

    @pl.when(has_next)
    def _():
        for copy in sent[-DEPTH:]:
            copy.wait_send()

    to_inner.wait_send()

    @pl.when(has_outer)
    def _():
        to_outer.wait_send()

    @pl.when(relays)
    def _():
        from_relay.wait_send()


def body(echoes, pair_list, phase_ramps):
    acqs, _, lines, width = echoes.shape
    groups = lines // LINES
    outputs = width // STEP
    chunks = chunk_list(groups)
    sizes = (acqs, groups, width, lax.axis_size("acq"), lax.axis_size("strip"))
    dma = pltpu.SemaphoreType.DMA
    look = pltpu.VMEM((acqs, 4, LINES, outputs), F32)
    return pl.pallas_call(
        functools.partial(kernel, sizes),
        out_shape=jax.ShapeDtypeStruct((acqs, 2, lines, outputs), F32),
        in_specs=[pl.BlockSpec(memory_space=pl.ANY)] * 3,
        out_specs=pl.BlockSpec(memory_space=pltpu.VMEM),
        scratch_shapes=[
            [pltpu.VMEM((2 * acqs - 1, 2, LINES, c[2]), F32) for c in chunks],
            pltpu.SMEM((2, acqs), I32),
            pltpu.SMEM((2, acqs), I32),
            pltpu.VMEM((width, 2 * outputs), BF16),
            pltpu.VMEM((acqs, 2, LINES, width), F32),
            pltpu.VMEM((acqs, 2, lines, outputs), F32),
            pltpu.VMEM((2 * acqs * 4 * LINES, max(c[2] for c in chunks)), BF16),
            pltpu.VMEM((acqs * 4 * LINES, outputs), F32),
            pltpu.VMEM((acqs, 2, lines, 2 * outputs), F32),
            [look for _ in range(groups)],
            pltpu.VMEM((2, acqs, 4, LINES, outputs), F32),
            look,
            dma((len(chunks),)),
            dma((len(chunks),)),
            dma((len(chunks),)),
            dma((2,)),
            dma((3,)),
            dma((2,)),
            dma((1,)),
        ],
        compiler_params=pltpu.CompilerParams(collective_id=0, has_side_effects=True, vmem_limit_bytes=16 << 20),
    )(*(pltpu.with_memory_space_constraint(v, pltpu.HBM) for v in (echoes, pair_list.T, phase_ramps.T)))


def solution(mesh):
    return jax.shard_map(
        body,
        mesh=mesh,
        in_specs=(P("acq", None, "strip", None), P("acq", None), P("acq", None)),
        out_specs=P("acq", None, "strip", None),
        check_vma=False,
    )
```

time: 25.6 us -> 23.6 us (0.922)
  the two profiles are of different devices: /device:TPU:103 before, /device:TPU:140 now
where the time goes in v3:
time: 23.6 us; the launch traced here: 23.5 us
  Pallas kernels  22.9 us (97%)
  local copies, waits for them, and re-layouts  0.66 us (3%)
    pallas_call x1, Pallas kernels, body(): pl.pallas_call(functools.partial(kernel, sizes), out_shape=jax.ShapeDtype...  22.9 us
    unnamed x1, local copies, waits for them, and re-layouts  0.66 us

profile of v3, /device:TPU:140, one launch (start us, length us, event | category | flops | bytes accessed | tf_op | source)
XLA Modules:
  0.0 23.5 jit_solution(6325828676404597975)
XLA Ops:
  0.0 22.9 %shard_map.37 = f32[4,2,32,128]{3,2,1,0:T(8,128)S(1)} custom-call(f32[4,2,32,2048]{3,2,1,0:T(8,128)} %echoes.1, s32[2,4]{1,0:T(2,128)} %bitcast.2, s32[2,4]{1,0:T(2,128)} %bitcast.3), custom_call_target="tpu_custom_call" | custom-call | tf_op jit(solution)/shard_map/pallas_call | solution.py:323
  22.9 0.7 %copy.5 = f32[4,2,32,128]{3,2,1,0:T(8,128)} copy(f32[4,2,32,128]{3,2,1,0:T(8,128)S(1)} %shard_map.37) | data formatting | bytes 262144

commit v4 on v3

--- a/solution.py
+++ b/solution.py
@@ -14,6 +14,7 @@
 PARTS = (1024, 1024)
 LAST_PARTS = (1024, 768, 256)
 DEPTH = 3
+DETOUR_AT = 2
 RELAY_AT = 3
 CHIPS = 4
 STEP = 16
@@ -48,7 +49,7 @@
 def kernel(
     sizes, echoes, pairs, ramps, out, pieces, pair_mem, ramp_mem, weights, table, line_table, fields,
     sums, partial, looks, edges, relayed, send_sem, recv_sem, own_sem, small_sem, edge_send, edge_recv,
-    relay_recv,
+    relay_recv, detour_send, detour_ready,
 ):
     acqs, groups, width, acq_size, strip_size = sizes
     reach = acqs - 1
@@ -81,6 +82,10 @@
     relay_room = jnp.where(relays_down, 0, 1)
     chunks = chunk_list(groups)
 
+    long_from = acq_size // 2 - 1
+    detour = len(chunks) - 2
+    starts_detour, passes_detour = acq == long_from, acq == 0
+
     barrier = pltpu.get_barrier_semaphore()
 
     def greet(condition, target):
@@ -92,6 +97,7 @@
     greet(jnp.logical_not(crosses), {"strip": inner})
     greet(crosses, {"acq": acq - place, "strip": relay_in})
     greet(has_outer, {"strip": outer})
+    greet(starts_detour | (acq == long_from + 1), {"acq": jnp.int32(0)})
     greet(relays, {"acq": acq + from_place, "strip": relay_from})
 
     pair_copy = pltpu.make_async_copy(pairs, pair_mem, small_sem.at[0])
@@ -113,21 +119,34 @@
         )
         sent.append(
             pltpu.make_async_remote_copy(
-                region(1, g, start, count), pieces[i].at[pl.ds(0, reach)], send_sem.at[i], recv_sem.at[i],
-                device_id={"acq": acq + 1}, device_id_type=MESH,
+                pieces[i].at[pl.ds(acqs, reach)], pieces[i].at[pl.ds(0, reach)], send_sem.at[i], recv_sem.at[i],
+                device_id={"acq": jnp.where(starts_detour, 0, acq + 1) if i == detour else acq + 1},
+                device_id_type=MESH,
             )
         )
 
+    for copy in own:
+        copy.start()
+
     neighbours = 1 + sum(c.astype(I32) for c in (has_next, has_outer, relays))
+    neighbours += 2 * passes_detour.astype(I32)
     pl.semaphore_wait(barrier, neighbours)
+    for copy in own[:DEPTH]:
+        copy.wait()
+
+    @pl.when(passes_detour)
+    def _():
+        pl.semaphore_signal(
+            detour_ready, inc=1, device_id={"acq": jnp.int32(long_from)}, device_id_type=MESH
+        )
 
     @pl.when(has_next)
     def _():
         for copy in sent[:DEPTH]:
             copy.start()
 
-    for copy in own:
-        copy.start()
+    for copy in own[DEPTH:]:
+        copy.wait()
 
     @pl.loop(0, width // TILE)
     def _(t):
@@ -156,6 +175,11 @@
     def _():
         edges[outer_room] = jnp.zeros(edges.shape[1:], F32)
 
+    detour_on = pltpu.make_async_remote_copy(
+        pieces[detour].at[pl.ds(0, reach)], pieces[detour].at[pl.ds(0, reach)],
+        detour_send.at[0], recv_sem.at[detour],
+        device_id={"acq": jnp.int32(long_from + 1)}, device_id_type=MESH,
+    )
     slots = [jnp.clip(pair_mem[0, p] - acq * acqs + reach, 0, reach + acqs - 1) for p in range(acqs)]
     half = acqs * 4 * LINES
 
@@ -208,11 +232,21 @@
                 to_relay.wait_recv()
                 from_relay.start()
 
+        if i == DETOUR_AT:
+
+            @pl.when(starts_detour)
+            def _():
+                pl.semaphore_wait(detour_ready, 1)
+                sent[detour].start()
+
         if i + DEPTH < len(chunks):
 
             @pl.when(has_next)
             def _():
                 sent[i].wait_send()
+
+            @pl.when(has_next & jnp.logical_not(starts_detour) if i + DEPTH == detour else has_next)
+            def _():
                 sent[i + DEPTH].start()
 
         if i == len(chunks) - 2:
@@ -229,7 +263,12 @@
                 for k in range(0, 4, 2):
                     partial[p, k // 2] = azimuth(p, k, blocks, early_left)
 
-        own[i].wait()
+        if i == detour:
+
+            @pl.when(passes_detour)
+            def _():
+                sent[i].wait_recv()
+                detour_on.start()
 
         @pl.when(has_previous)
         def _():
@@ -300,6 +339,10 @@
     def _():
         for copy in sent[-DEPTH:]:
             copy.wait_send()
+
+    @pl.when(passes_detour)
+    def _():
+        detour_on.wait_send()
 
     to_inner.wait_send()
 
@@ -345,6 +388,8 @@
             dma((3,)),
             dma((2,)),
             dma((1,)),
+            dma((1,)),
+            pltpu.SemaphoreType.REGULAR,
         ],
         compiler_params=pltpu.CompilerParams(collective_id=0, has_side_effects=True, vmem_limit_bytes=16 << 20),
     )(*(pltpu.with_memory_space_constraint(v, pltpu.HBM) for v in (echoes, pair_list.T, phase_ramps.T)))

time: 23.6 us -> 22.9 us (0.970)
  the two profiles are of different devices: /device:TPU:140 before, /device:TPU:184 now
where the time goes in v4:
time: 22.9 us; the launch traced here: 22.8 us
  Pallas kernels  22.2 us (97%)
  local copies, waits for them, and re-layouts  0.66 us (3%)
    pallas_call x1, Pallas kernels, body(): pl.pallas_call(functools.partial(kernel, sizes), out_shape=jax.ShapeDtype...  22.2 us
    unnamed x1, local copies, waits for them, and re-layouts  0.66 us

profile of v4, /device:TPU:184, one launch (start us, length us, event | category | flops | bytes accessed | tf_op | source)
XLA Modules:
  0.0 22.8 jit_solution(11846182387979982539)
XLA Ops:
  0.0 22.2 %shard_map.37 = f32[4,2,32,128]{3,2,1,0:T(8,128)S(1)} custom-call(f32[4,2,32,2048]{3,2,1,0:T(8,128)} %echoes.1, s32[2,4]{1,0:T(2,128)} %bitcast.2, s32[2,4]{1,0:T(2,128)} %bitcast.3), custom_call_target="tpu_custom_call" | custom-call | tf_op jit(solution)/shard_map/pallas_call | solution.py:366
  22.2 0.7 %copy.5 = f32[4,2,32,128]{3,2,1,0:T(8,128)} copy(f32[4,2,32,128]{3,2,1,0:T(8,128)S(1)} %shard_map.37) | data formatting | bytes 262144

commit v5 on v4

--- a/solution.py
+++ b/solution.py
@@ -11,11 +11,11 @@
 MESH = pl.DeviceIdType.MESH
 F32, BF16, I32 = jnp.float32, jnp.bfloat16, jnp.int32
 LINES = 8
-PARTS = (1024, 1024)
+PARTS = (2048,)
 LAST_PARTS = (1024, 768, 256)
 DEPTH = 3
-DETOUR_AT = 2
-RELAY_AT = 3
+DETOUR_AT = 1
+RELAY_AT = 1
 CHIPS = 4
 STEP = 16
 TILE = 256
@@ -48,7 +48,7 @@
 
 def kernel(
     sizes, echoes, pairs, ramps, out, pieces, pair_mem, ramp_mem, weights, table, line_table, fields,
-    sums, partial, looks, edges, relayed, send_sem, recv_sem, own_sem, small_sem, edge_send, edge_recv,
+    sums, partial, looks, edges, relayed, send_sem, recv_sem, own_sem, edge_send, edge_recv,
     relay_recv, detour_send, detour_ready,
 ):
     acqs, groups, width, acq_size, strip_size = sizes
@@ -100,8 +100,8 @@
     greet(starts_detour | (acq == long_from + 1), {"acq": jnp.int32(0)})
     greet(relays, {"acq": acq + from_place, "strip": relay_from})
 
-    pair_copy = pltpu.make_async_copy(pairs, pair_mem, small_sem.at[0])
-    ramp_copy = pltpu.make_async_copy(ramps, ramp_mem, small_sem.at[1])
+    pair_copy = pltpu.make_async_copy(pairs, pair_mem, edge_send.at[0])
+    ramp_copy = pltpu.make_async_copy(ramps, ramp_mem, edge_send.at[1])
     pair_copy.start()
     ramp_copy.start()
 
@@ -114,25 +114,24 @@
     for i, (g, start, count, _, _) in enumerate(chunks):
         own.append(
             pltpu.make_async_copy(
-                region(0, g, start, count), pieces[i].at[pl.ds(reach, acqs)], own_sem.at[i]
+                region(0, g, start, count), pieces[i].at[pl.ds(reach, acqs)], own_sem.at[i % DEPTH]
             )
         )
         sent.append(
             pltpu.make_async_remote_copy(
-                pieces[i].at[pl.ds(acqs, reach)], pieces[i].at[pl.ds(0, reach)], send_sem.at[i], recv_sem.at[i],
+                pieces[i].at[pl.ds(acqs, reach)], pieces[i].at[pl.ds(0, reach)],
+                detour_send.at[0] if i == detour else send_sem.at[i % DEPTH], recv_sem.at[i],
                 device_id={"acq": jnp.where(starts_detour, 0, acq + 1) if i == detour else acq + 1},
                 device_id_type=MESH,
             )
         )
 
-    for copy in own:
+    for copy in own[:DEPTH]:
         copy.start()
 
     neighbours = 1 + sum(c.astype(I32) for c in (has_next, has_outer, relays))
     neighbours += 2 * passes_detour.astype(I32)
     pl.semaphore_wait(barrier, neighbours)
-    for copy in own[:DEPTH]:
-        copy.wait()
 
     @pl.when(passes_detour)
     def _():
@@ -140,13 +139,15 @@
             detour_ready, inc=1, device_id={"acq": jnp.int32(long_from)}, device_id_type=MESH
         )
 
-    @pl.when(has_next)
-    def _():
-        for copy in sent[:DEPTH]:
-            copy.start()
-
-    for copy in own[DEPTH:]:
-        copy.wait()
+    for i in range(DEPTH):
+        own[i].wait()
+
+        @pl.when(has_next)
+        def _():
+            sent[i].start()
+
+        if i + DEPTH < len(chunks):
+            own[i + DEPTH].start()
 
     @pl.loop(0, width // TILE)
     def _(t):
@@ -177,7 +178,7 @@
 
     detour_on = pltpu.make_async_remote_copy(
         pieces[detour].at[pl.ds(0, reach)], pieces[detour].at[pl.ds(0, reach)],
-        detour_send.at[0], recv_sem.at[detour],
+        detour_send.at[1], recv_sem.at[detour],
         device_id={"acq": jnp.int32(long_from + 1)}, device_id_type=MESH,
     )
     slots = [jnp.clip(pair_mem[0, p] - acq * acqs + reach, 0, reach + acqs - 1) for p in range(acqs)]
@@ -232,6 +233,9 @@
                 to_relay.wait_recv()
                 from_relay.start()
 
+        if i + DEPTH < len(chunks):
+            own[i + DEPTH].wait()
+
         if i == DETOUR_AT:
 
             @pl.when(starts_detour)
@@ -240,7 +244,6 @@
                 sent[detour].start()
 
         if i + DEPTH < len(chunks):
-
             @pl.when(has_next)
             def _():
                 sent[i].wait_send()
@@ -381,14 +384,13 @@
             [look for _ in range(groups)],
             pltpu.VMEM((2, acqs, 4, LINES, outputs), F32),
             look,
+            dma((DEPTH,)),
             dma((len(chunks),)),
-            dma((len(chunks),)),
-            dma((len(chunks),)),
-            dma((2,)),
+            dma((DEPTH,)),
             dma((3,)),
             dma((2,)),
             dma((1,)),
-            dma((1,)),
+            dma((2,)),
             pltpu.SemaphoreType.REGULAR,
         ],
         compiler_params=pltpu.CompilerParams(collective_id=0, has_side_effects=True, vmem_limit_bytes=16 << 20),

time: 22.9 us -> 22.8 us (level)
  no operation moved by 1% of the time
where the time goes in v5:
time: 22.8 us; the launch traced here: 22.7 us
  Pallas kernels  22 us (96%)
  local copies, waits for them, and re-layouts  0.66 us (3%)
    pallas_call x1, Pallas kernels, body(): pl.pallas_call(functools.partial(kernel, sizes), out_shape=jax.ShapeDtype...  22 us
    unnamed x1, local copies, waits for them, and re-layouts  0.66 us

profile of v5, /device:TPU:184, one launch (start us, length us, event | category | flops | bytes accessed | tf_op | source)
XLA Modules:
  0.0 22.7 jit_solution(8478706440593769451)
XLA Ops:
  0.0 22.0 %shard_map.37 = f32[4,2,32,128]{3,2,1,0:T(8,128)S(1)} custom-call(f32[4,2,32,2048]{3,2,1,0:T(8,128)} %echoes.1, s32[2,4]{1,0:T(2,128)} %bitcast.2, s32[2,4]{1,0:T(2,128)} %bitcast.3), custom_call_target="tpu_custom_call" | custom-call | tf_op jit(solution)/shard_map/pallas_call | solution.py:369
  22.0 0.7 %copy.5 = f32[4,2,32,128]{3,2,1,0:T(8,128)} copy(f32[4,2,32,128]{3,2,1,0:T(8,128)S(1)} %shard_map.37) | data formatting | bytes 262144

commit v6 on v5

--- a/solution.py
+++ b/solution.py
@@ -50,6 +50,7 @@
     sizes, echoes, pairs, ramps, out, pieces, pair_mem, ramp_mem, weights, table, line_table, fields,
     sums, partial, looks, edges, relayed, send_sem, recv_sem, own_sem, edge_send, edge_recv,
     relay_recv, detour_send, detour_ready,
+    relay_ready,
 ):
     acqs, groups, width, acq_size, strip_size = sizes
     reach = acqs - 1
@@ -98,7 +99,7 @@
     greet(crosses, {"acq": acq - place, "strip": relay_in})
     greet(has_outer, {"strip": outer})
     greet(starts_detour | (acq == long_from + 1), {"acq": jnp.int32(0)})
-    greet(relays, {"acq": acq + from_place, "strip": relay_from})
+    greet(crosses, {"acq": acq - place, "strip": relay_out})
 
     pair_copy = pltpu.make_async_copy(pairs, pair_mem, edge_send.at[0])
     ramp_copy = pltpu.make_async_copy(ramps, ramp_mem, edge_send.at[1])
@@ -129,15 +130,10 @@
     for copy in own[:DEPTH]:
         copy.start()
 
-    neighbours = 1 + sum(c.astype(I32) for c in (has_next, has_outer, relays))
+    waits = (has_next, has_outer, jnp.logical_not(crosses), relays, relays)
+    neighbours = sum(c.astype(I32) for c in waits)
     neighbours += 2 * passes_detour.astype(I32)
     pl.semaphore_wait(barrier, neighbours)
-
-    @pl.when(passes_detour)
-    def _():
-        pl.semaphore_signal(
-            detour_ready, inc=1, device_id={"acq": jnp.int32(long_from)}, device_id_type=MESH
-        )
 
     for i in range(DEPTH):
         own[i].wait()
@@ -148,6 +144,19 @@
 
         if i + DEPTH < len(chunks):
             own[i + DEPTH].start()
+
+    @pl.when(relays)
+    def _():
+        pl.semaphore_signal(
+            relay_ready, inc=1, device_id={"acq": acq + from_place, "strip": relay_from},
+            device_id_type=MESH,
+        )
+
+    @pl.when(passes_detour)
+    def _():
+        pl.semaphore_signal(
+            detour_ready, inc=1, device_id={"acq": jnp.int32(long_from)}, device_id_type=MESH
+        )
 
     @pl.loop(0, width // TILE)
     def _(t):
@@ -317,6 +326,7 @@
 
                 @pl.when(crosses)
                 def _():
+                    pl.semaphore_wait(relay_ready, 1)
                     to_relay.start()
 
                 @pl.when(jnp.logical_not(crosses))
@@ -392,6 +402,7 @@
             dma((1,)),
             dma((2,)),
             pltpu.SemaphoreType.REGULAR,
+            pltpu.SemaphoreType.REGULAR,
         ],
         compiler_params=pltpu.CompilerParams(collective_id=0, has_side_effects=True, vmem_limit_bytes=16 << 20),
     )(*(pltpu.with_memory_space_constraint(v, pltpu.HBM) for v in (echoes, pair_list.T, phase_ramps.T)))

time: 22.8 us -> 22.3 us (0.978)
  Pallas kernels: 22 us -> 21.3 us
    pallas_call x1, Pallas kernels: 22 us -> 21.3 us  [body(): pl.pallas_call(functools.partial(kernel, sizes), out_shape=jax.ShapeDtype...]
where the time goes in v6:
time: 22.3 us; the launch traced here: 22 us
  Pallas kernels  21.3 us (96%)
  local copies, waits for them, and re-layouts  0.66 us (3%)
    pallas_call x1, Pallas kernels, body(): pl.pallas_call(functools.partial(kernel, sizes), out_shape=jax.ShapeDtype...  21.3 us
    unnamed x1, local copies, waits for them, and re-layouts  0.66 us

profile of v6, /device:TPU:184, one launch (start us, length us, event | category | flops | bytes accessed | tf_op | source)
XLA Modules:
  0.0 22.0 jit_solution(7902570910568982013)
XLA Ops:
  0.0 21.3 %shard_map.37 = f32[4,2,32,128]{3,2,1,0:T(8,128)S(1)} custom-call(f32[4,2,32,2048]{3,2,1,0:T(8,128)} %echoes.1, s32[2,4]{1,0:T(2,128)} %bitcast.2, s32[2,4]{1,0:T(2,128)} %bitcast.3), custom_call_target="tpu_custom_call" | custom-call | tf_op jit(solution)/shard_map/pallas_call | solution.py:379
  21.3 0.7 %copy.5 = f32[4,2,32,128]{3,2,1,0:T(8,128)} copy(f32[4,2,32,128]{3,2,1,0:T(8,128)S(1)} %shard_map.37) | data formatting | bytes 262144

commit v7 on v6

--- a/solution.py
+++ b/solution.py
@@ -15,6 +15,7 @@
 LAST_PARTS = (1024, 768, 256)
 DEPTH = 3
 DETOUR_AT = 1
+PASS_AT = 3
 RELAY_AT = 1
 CHIPS = 4
 STEP = 16
@@ -235,6 +236,13 @@
     late_left = azimuth_left(first_line[-1:])
 
     for i, (g, start, count, first_part, last_part) in enumerate(chunks):
+        if i == PASS_AT:
+
+            @pl.when(passes_detour)
+            def _():
+                sent[detour].wait_recv()
+                detour_on.start()
+
         if i == RELAY_AT:
 
             @pl.when(relays)
@@ -274,13 +282,6 @@
             for p in range(acqs):
                 for k in range(0, 4, 2):
                     partial[p, k // 2] = azimuth(p, k, blocks, early_left)
-
-        if i == detour:
-
-            @pl.when(passes_detour)
-            def _():
-                sent[i].wait_recv()
-                detour_on.start()
 
         @pl.when(has_previous)
         def _():

time: 22.3 us -> 22.1 us (level)
  no operation moved by 1% of the time
where the time goes in v7:
time: 22.1 us; the launch traced here: 22 us
  Pallas kernels  21.3 us (96%)
  local copies, waits for them, and re-layouts  0.66 us (3%)
    pallas_call x1, Pallas kernels, body(): pl.pallas_call(functools.partial(kernel, sizes), out_shape=jax.ShapeDtype...  21.3 us
    unnamed x1, local copies, waits for them, and re-layouts  0.66 us

profile of v7, /device:TPU:184, one launch (start us, length us, event | category | flops | bytes accessed | tf_op | source)
XLA Modules:
  0.0 22.0 jit_solution(3280844329190833919)
XLA Ops:
  0.0 21.3 %shard_map.37 = f32[4,2,32,128]{3,2,1,0:T(8,128)S(1)} custom-call(f32[4,2,32,2048]{3,2,1,0:T(8,128)} %echoes.1, s32[2,4]{1,0:T(2,128)} %bitcast.2, s32[2,4]{1,0:T(2,128)} %bitcast.3), custom_call_target="tpu_custom_call" | custom-call | tf_op jit(solution)/shard_map/pallas_call | solution.py:380
  21.3 0.7 %copy.5 = f32[4,2,32,128]{3,2,1,0:T(8,128)} copy(f32[4,2,32,128]{3,2,1,0:T(8,128)S(1)} %shard_map.37) | data formatting | bytes 262144

commit v8 on v7

--- a/solution.py
+++ b/solution.py
@@ -188,7 +188,7 @@
 
     detour_on = pltpu.make_async_remote_copy(
         pieces[detour].at[pl.ds(0, reach)], pieces[detour].at[pl.ds(0, reach)],
-        detour_send.at[1], recv_sem.at[detour],
+        own_sem.at[0], recv_sem.at[detour],
         device_id={"acq": jnp.int32(long_from + 1)}, device_id_type=MESH,
     )
     slots = [jnp.clip(pair_mem[0, p] - acq * acqs + reach, 0, reach + acqs - 1) for p in range(acqs)]
@@ -345,7 +345,7 @@
         for k in range(0, 4, 2):
             value = partial[p, k // 2] + azimuth(p, k, looks[-1:], late_left)
             summed += [value[:, :outputs], value[:, outputs:]]
-        scaling = 1.0 / jnp.sqrt(summed[2] * summed[3] + 1e-06)
+        scaling = lax.rsqrt(summed[2] * summed[3] + 1e-06)
         out[p, 0] = summed[0] * scaling
         out[p, 1] = summed[1] * scaling
 
@@ -401,7 +401,7 @@
             dma((3,)),
             dma((2,)),
             dma((1,)),
-            dma((2,)),
+            dma((1,)),
             pltpu.SemaphoreType.REGULAR,
             pltpu.SemaphoreType.REGULAR,
         ],

time: 22.1 us -> 22.1 us (level)
  no operation moved by 1% of the time
where the time goes in v8:
time: 22.1 us; the launch traced here: 22 us
  Pallas kernels  21.3 us (96%)
  local copies, waits for them, and re-layouts  0.66 us (3%)
    pallas_call x1, Pallas kernels, body(): pl.pallas_call(functools.partial(kernel, sizes), out_shape=jax.ShapeDtype...  21.3 us
    unnamed x1, local copies, waits for them, and re-layouts  0.66 us

profile of v8, /device:TPU:184, one launch (start us, length us, event | category | flops | bytes accessed | tf_op | source)
XLA Modules:
  0.0 22.0 jit_solution(599843975893634175)
XLA Ops:
  0.0 21.3 %shard_map.37 = f32[4,2,32,128]{3,2,1,0:T(8,128)S(1)} custom-call(f32[4,2,32,2048]{3,2,1,0:T(8,128)} %echoes.1, s32[2,4]{1,0:T(2,128)} %bitcast.2, s32[2,4]{1,0:T(2,128)} %bitcast.3), custom_call_target="tpu_custom_call" | custom-call | tf_op jit(solution)/shard_map/pallas_call | solution.py:380
  21.3 0.7 %copy.5 = f32[4,2,32,128]{3,2,1,0:T(8,128)} copy(f32[4,2,32,128]{3,2,1,0:T(8,128)S(1)} %shard_map.37) | data formatting | bytes 262144

commit v9 on v8

--- a/solution.py
+++ b/solution.py
@@ -232,6 +232,7 @@
         high = taps.astype(BF16).astype(F32)
         return jnp.concatenate([high, high, taps - high], axis=1).astype(BF16)
 
+    late = {}
     early_left = azimuth_left([-LINES, lines, *first_line[:-1]])
     late_left = azimuth_left(first_line[-1:])
 
@@ -315,14 +316,15 @@
         if last_part:
             whole = part if first_part else sums[...] + part
             whole = whole.reshape(acqs, 4, LINES, outputs)
+            room = late if g == groups - 1 else looks[g]
             for p in range(acqs):
                 now = pl.ds(first_line[g], LINES)
                 cosine, sine = line_table[p, 0, now, :], line_table[p, 1, now, :]
                 x, y = whole[p, 0], whole[p, 1]
-                looks[g][p, 0] = x * cosine + y * sine
-                looks[g][p, 1] = y * cosine - x * sine
-                looks[g][p, 2] = whole[p, 2]
-                looks[g][p, 3] = whole[p, 3]
+                room[p, 0] = x * cosine + y * sine
+                room[p, 1] = y * cosine - x * sine
+                room[p, 2] = whole[p, 2]
+                room[p, 3] = whole[p, 3]
             if g == 0:
 
                 @pl.when(crosses)
@@ -343,7 +345,7 @@
     for p in range(acqs):
         summed = []
         for k in range(0, 4, 2):
-            value = partial[p, k // 2] + azimuth(p, k, looks[-1:], late_left)
+            value = partial[p, k // 2] + azimuth(p, k, [late], late_left)
             summed += [value[:, :outputs], value[:, outputs:]]
         scaling = lax.rsqrt(summed[2] * summed[3] + 1e-06)
         out[p, 0] = summed[0] * scaling

time: 22.1 us -> 22.1 us (level)
  no operation moved by 1% of the time
where the time goes in v9:
time: 22.1 us; the launch traced here: 22 us
  Pallas kernels  21.3 us (96%)
  local copies, waits for them, and re-layouts  0.66 us (3%)
    pallas_call x1, Pallas kernels, body(): pl.pallas_call(functools.partial(kernel, sizes), out_shape=jax.ShapeDtype...  21.3 us
    unnamed x1, local copies, waits for them, and re-layouts  0.66 us

profile of v9, /device:TPU:184, one launch (start us, length us, event | category | flops | bytes accessed | tf_op | source)
XLA Modules:
  0.0 22.0 jit_solution(599843975893634175)
XLA Ops:
  0.0 21.3 %shard_map.37 = f32[4,2,32,128]{3,2,1,0:T(8,128)S(1)} custom-call(f32[4,2,32,2048]{3,2,1,0:T(8,128)} %echoes.1, s32[2,4]{1,0:T(2,128)} %bitcast.2, s32[2,4]{1,0:T(2,128)} %bitcast.3), custom_call_target="tpu_custom_call" | custom-call | tf_op jit(solution)/shard_map/pallas_call | solution.py:382
  21.3 0.7 %copy.5 = f32[4,2,32,128]{3,2,1,0:T(8,128)} copy(f32[4,2,32,128]{3,2,1,0:T(8,128)S(1)} %shard_map.37) | data formatting | bytes 262144
